TPU v7x, 32 devices: a whole 2x2x4 slice. The times are simulated.
32 devices in a mesh: wide: 8 (over y, x, core), narrow: 4 (over z).
Axes of the slice: x: 2, y: 2, z: 4, core: 2. Of those that a mesh axis runs over, the one named last changes fastest.
Arguments:
- query_tokens: bfloat16 [4096, 768], P(('wide', 'narrow')), may hold values from -6 to 6
- passage_tokens: bfloat16 [12288, 768], P(('wide', 'narrow')), may hold values from -6 to 6
- query_cotangent: bfloat16 [4096, 768], P(('wide', 'narrow')), may hold values from -6 to 6
- passage_cotangent: bfloat16 [12288, 768], P(('wide', 'narrow')), may hold values from -6 to 6
- query_segments: int32 [8, 512], P('wide'), may hold values from -1 to 15, as said below
- passage_segments: int32 [24, 512], P('wide'), may hold values from -1 to 3, as said below
- query_cls: int32 [8, 16], P('wide'), may hold values from 0 to 485, as said below
- passage_cls: int32 [24, 4], P('wide'), may hold values from 0 to 485, as said below
- query_weight: bfloat16 [2, 768, 768], P(None, None, 'narrow'), may hold values from -0.3125 to 0.3125
- query_bias: float32 [2, 768], P(None, 'narrow'), may hold values from -3 to 3
- key_weight: bfloat16 [2, 768, 768], P(None, None, 'narrow'), may hold values from -0.3125 to 0.3125
- value_weight: bfloat16 [2, 768, 768], P(None, None, 'narrow'), may hold values from -0.21875 to 0.21875
- value_bias: float32 [2, 768], P(None, 'narrow'), may hold values from -3 to 3
- out_weight: bfloat16 [2, 768, 768], P(None, 'narrow'), may hold values from -1.25 to 1.25
- out_bias: float32 [2, 768], replicated, may hold values from -3 to 3
- norm1_gain: float32 [2, 768], replicated, may hold values from 0.25 to 1.75
- norm1_bias: float32 [2, 768], replicated, may hold values from -3 to 3
- inner_weight: bfloat16 [2, 768, 3072], P(None, None, 'narrow'), may hold values from -0.21875 to 0.21875
- inner_bias: float32 [2, 3072], P(None, 'narrow'), may hold values from -3 to 3
- outer_weight: bfloat16 [2, 3072, 768], P(None, 'narrow'), may hold values from -0.109375 to 0.109375
- outer_bias: float32 [2, 768], replicated, may hold values from -3 to 3
- norm2_gain: float32 [2, 768], replicated, may hold values from 0.25 to 1.75
- norm2_bias: float32 [2, 768], replicated, may hold values from -3 to 3
Outputs:
- query_out: bfloat16 [4096, 768], P(('wide', 'narrow'))
- passage_out: bfloat16 [12288, 768], P(('wide', 'narrow'))
- query_grad_in: bfloat16 [4096, 768], P(('wide', 'narrow'))
- passage_grad_in: bfloat16 [12288, 768], P(('wide', 'narrow'))
- query_pooled: bfloat16 [8, 16, 768], P('wide', None, 'narrow')
- passage_pooled: bfloat16 [24, 4, 768], P('wide', None, 'narrow')
- grad_query_weight: float32 [2, 768, 768], P(None, None, 'narrow')
- grad_query_bias: float32 [2, 768], P(None, 'narrow')
- grad_key_weight: float32 [2, 768, 768], P(None, None, 'narrow')
- grad_value_weight: float32 [2, 768, 768], P(None, None, 'narrow')
- grad_value_bias: float32 [2, 768], P(None, 'narrow')
- grad_out_weight: float32 [2, 768, 768], P(None, 'narrow')
- grad_out_bias: float32 [2, 768], replicated
- grad_norm1_gain: float32 [2, 768], replicated
- grad_norm1_bias: float32 [2, 768], replicated
- grad_inner_weight: float32 [2, 768, 3072], P(None, None, 'narrow')
- grad_inner_bias: float32 [2, 3072], P(None, 'narrow')
- grad_outer_weight: float32 [2, 3072, 768], P(None, 'narrow')
- grad_outer_bias: float32 [2, 768], replicated
- grad_norm2_gain: float32 [2, 768], replicated
- grad_norm2_bias: float32 [2, 768], replicated
Inputs may be any that keep to these rules, and one draw needn't show every extreme that they name: `query_segments`: segment numbers never fall along a row and rise by one from 0 at each segment's first token; every segment spans 2 or more tokens; -1 marks padding at the end of every row. `passage_segments`: as for query_segments. query_cls[r, j] is the first position of segment j in row r of query_segments. passage_cls[r, j] is the first position of segment j in row r of passage_segments.
All inputs are finite; a program needn't handle non-finite values.
Results may differ from a plain program's by a relative error of at most 0.018.
The roundings to bfloat16 on the way count: a program that leaves them out, or rounds other values in their place, can miss the bound.
Values may be sent and summed in bfloat16 or wider, within the bound.
No kernel may reach another device: no remote copies, remote signals or barrier semaphores. Data moves between devices by JAX's collectives and lax.ppermute only.
A program may use at most 128 MiB of HBM per device.

v0:
```python
import math
import jax
import jax.numpy as jnp
from jax import lax
from jax.sharding import PartitionSpec as P

HDIM = 64
NORM_EPS = 1e-05
MASKED = -1e30


def matmul(left, right):
    return jnp.dot(left, right, preferred_element_type=jnp.float32)


def matmul_left(left, right):
    return lax.dot_general(
        left, right, (((0,), (0,)), ((), ())), preferred_element_type=jnp.float32
    )


def matmul_right(left, right):
    return lax.dot_general(
        left, right, (((1,), (1,)), ((), ())), preferred_element_type=jnp.float32
    )


def layer_norm(values, gain, bias):
    centred = values - jnp.mean(values, -1, keepdims=True)
    inverse = lax.rsqrt(jnp.mean(centred * centred, -1, keepdims=True) + NORM_EPS)
    normed = centred * inverse
    return (normed * gain + bias, normed, inverse)


def norm_back(upstream, normed, inverse, gain):
    scaled = upstream * gain
    return inverse * (
        scaled
        - jnp.mean(scaled, -1, keepdims=True)
        - normed * jnp.mean(scaled * normed, -1, keepdims=True)
    )


def gelu_slope(values):
    return 0.5 * (1.0 + lax.erf(values * (1.0 / math.sqrt(2.0)))) + values * jnp.exp(
        -0.5 * values * values
    ) * (1.0 / math.sqrt(2.0 * math.pi))


def counted(labels):
    return ((labels[:, None] == labels[None, :]) & (labels[None, :] >= 0))[None]


def attend(block, scaling):
    queries, key_vecs, value_vecs, labels = block
    scores = (
        jnp.einsum("qhd,khd->hqk", queries, key_vecs, preferred_element_type=jnp.float32) * scaling
    )
    allowed = counted(labels)
    row_top = jnp.max(jnp.where(allowed, scores, MASKED), -1, keepdims=True)
    unnorm = jnp.exp(jnp.where(allowed, scores - row_top, MASKED))
    totals = jnp.maximum(jnp.sum(unnorm, -1, keepdims=True), 1.0)
    probs = (unnorm / totals).astype(jnp.bfloat16)
    attended = jnp.einsum("hqk,khd->qhd", probs, value_vecs, preferred_element_type=jnp.float32)
    return (attended, row_top + jnp.log(totals))


def attend_back(block, scaling):
    queries, key_vecs, value_vecs, labels, log_total, upstream = block
    scores = (
        jnp.einsum("qhd,khd->hqk", queries, key_vecs, preferred_element_type=jnp.float32) * scaling
    )
    allowed = counted(labels)
    probs = jnp.exp(jnp.where(allowed, scores - log_total, MASKED))
    grad_value = jnp.einsum(
        "hqk,qhd->khd", probs.astype(jnp.bfloat16), upstream, preferred_element_type=jnp.float32
    )
    grad_probs = jnp.einsum(
        "qhd,khd->hqk", upstream, value_vecs, preferred_element_type=jnp.float32
    )
    grad_scores = (probs * (grad_probs - jnp.sum(probs * grad_probs, -1, keepdims=True))).astype(
        jnp.bfloat16
    )
    grad_query = (
        jnp.einsum("hqk,khd->qhd", grad_scores, key_vecs, preferred_element_type=jnp.float32)
        * scaling
    )
    grad_key = (
        jnp.einsum("hqk,qhd->khd", grad_scores, queries, preferred_element_type=jnp.float32)
        * scaling
    )
    return (grad_query, grad_key, grad_value)


def tower(tokens, cotangent, labels, cls_pos, weights, tower_index):
    (
        query_weight,
        query_bias,
        key_weight,
        value_weight,
        value_bias,
        out_weight,
        out_bias,
        norm1_gain,
        norm1_bias,
        inner_weight,
        inner_bias,
        outer_weight,
        outer_bias,
        norm2_gain,
        norm2_bias,
    ) = [member[tower_index] for member in weights]
    shard_rows = tokens.shape[0]
    seq_count, length = labels.shape
    head_cols = query_weight.shape[1]
    heads_here = head_cols // HDIM
    scaling = HDIM ** (-0.5)
    split_shape = (seq_count, length, heads_here, HDIM)
    full_rows = lax.all_gather(tokens, "narrow", axis=0, tiled=True)
    joined = jnp.concatenate([query_weight, key_weight, value_weight], 1)
    projected = matmul(full_rows, joined)
    queries = (projected[:, :head_cols] + query_bias).astype(jnp.bfloat16).reshape(split_shape)
    key_vecs = projected[:, head_cols : 2 * head_cols].astype(jnp.bfloat16).reshape(split_shape)
    value_vecs = (
        (projected[:, 2 * head_cols :] + value_bias).astype(jnp.bfloat16).reshape(split_shape)
    )
    attended, log_total = lax.map(
        lambda block: attend(block, scaling), (queries, key_vecs, value_vecs, labels)
    )
    attended = attended.reshape(-1, head_cols).astype(jnp.bfloat16)
    attn_out = lax.psum_scatter(
        matmul(attended, out_weight), "narrow", scatter_dimension=0, tiled=True
    )
    hidden1, normed1, inverse1 = layer_norm(
        tokens.astype(jnp.float32) + attn_out + out_bias, norm1_gain, norm1_bias
    )
    hidden_full = lax.all_gather(hidden1.astype(jnp.bfloat16), "narrow", axis=0, tiled=True)
    inner_pre = matmul(hidden_full, inner_weight) + inner_bias
    activated = jax.nn.gelu(inner_pre, approximate=False).astype(jnp.bfloat16)
    ffn_out = lax.psum_scatter(
        matmul(activated, outer_weight), "narrow", scatter_dimension=0, tiled=True
    )
    result, normed2, inverse2 = layer_norm(hidden1 + ffn_out + outer_bias, norm2_gain, norm2_bias)
    result = result.astype(jnp.bfloat16)
    cls_tokens = (cls_pos + jnp.arange(seq_count, dtype=jnp.int32)[:, None] * length).reshape(-1)
    here_rows = lax.axis_index("narrow") * shard_rows + jnp.arange(shard_rows, dtype=jnp.int32)
    picked = (cls_tokens[:, None] == here_rows[None, :]).astype(jnp.bfloat16)
    pooled_part = matmul(picked, result).reshape(seq_count, cls_pos.shape[1], -1)
    pooled = lax.psum_scatter(
        pooled_part.astype(jnp.bfloat16), "narrow", scatter_dimension=2, tiled=True
    )
    cot_rows = cotangent.astype(jnp.float32)
    grad_gain2 = jnp.sum(cot_rows * normed2, 0)
    grad_bias2 = jnp.sum(cot_rows, 0)
    grad_resid2 = norm_back(cot_rows, normed2, inverse2, norm2_gain)
    grad_outer_bias = jnp.sum(grad_resid2, 0)
    resid2_full = lax.all_gather(grad_resid2.astype(jnp.bfloat16), "narrow", axis=0, tiled=True)
    grad_outer_weight = matmul_left(activated, resid2_full)
    grad_act = matmul_right(resid2_full, outer_weight)
    grad_inner = (grad_act * gelu_slope(inner_pre)).astype(jnp.bfloat16)
    grad_inner_weight = matmul_left(hidden_full, grad_inner)
    grad_inner_bias = jnp.sum(grad_inner, 0, dtype=jnp.float32)
    grad_hidden1 = (
        lax.psum_scatter(
            matmul_right(grad_inner, inner_weight), "narrow", scatter_dimension=0, tiled=True
        )
        + grad_resid2
    )
    grad_gain1 = jnp.sum(grad_hidden1 * normed1, 0)
    grad_bias1 = jnp.sum(grad_hidden1, 0)
    grad_resid1 = norm_back(grad_hidden1, normed1, inverse1, norm1_gain)
    grad_out_bias = jnp.sum(grad_resid1, 0)
    resid1_full = lax.all_gather(grad_resid1.astype(jnp.bfloat16), "narrow", axis=0, tiled=True)
    grad_out_weight = matmul_left(attended, resid1_full)
    grad_attended = matmul_right(resid1_full, out_weight).astype(jnp.bfloat16).reshape(split_shape)
    grad_query, grad_key, grad_value = lax.map(
        lambda block: attend_back(block, scaling),
        (queries, key_vecs, value_vecs, labels, log_total, grad_attended),
    )
    grad_proj = jnp.concatenate(
        [
            grad_query.reshape(-1, head_cols),
            grad_key.reshape(-1, head_cols),
            grad_value.reshape(-1, head_cols),
        ],
        1,
    ).astype(jnp.bfloat16)
    grad_joined = matmul_left(full_rows, grad_proj)
    grad_query_bias = jnp.sum(grad_proj[:, :head_cols], 0, dtype=jnp.float32)
    grad_value_bias = jnp.sum(grad_proj[:, 2 * head_cols :], 0, dtype=jnp.float32)
    grad_in = (
        lax.psum_scatter(
            matmul_right(grad_proj, joined).astype(jnp.bfloat16),
            "narrow",
            scatter_dimension=0,
            tiled=True,
        ).astype(jnp.float32)
        + grad_resid1
    ).astype(jnp.bfloat16)
    big_grads = (
        grad_joined[:, :head_cols],
        grad_query_bias,
        grad_joined[:, head_cols : 2 * head_cols],
        grad_joined[:, 2 * head_cols :],
        grad_value_bias,
        grad_out_weight,
        grad_inner_weight,
        grad_inner_bias,
        grad_outer_weight,
    )
    small_grads = (grad_out_bias, grad_gain1, grad_bias1, grad_outer_bias, grad_gain2, grad_bias2)
    return (result, grad_in, pooled, big_grads, small_grads)


def per_device(
    query_tokens,
    passage_tokens,
    query_cotangent,
    passage_cotangent,
    query_segments,
    passage_segments,
    query_cls,
    passage_cls,
    query_weight,
    query_bias,
    key_weight,
    value_weight,
    value_bias,
    out_weight,
    out_bias,
    norm1_gain,
    norm1_bias,
    inner_weight,
    inner_bias,
    outer_weight,
    outer_bias,
    norm2_gain,
    norm2_bias,
):
    weights = (
        query_weight,
        query_bias,
        key_weight,
        value_weight,
        value_bias,
        out_weight,
        out_bias,
        norm1_gain,
        norm1_bias,
        inner_weight,
        inner_bias,
        outer_weight,
        outer_bias,
        norm2_gain,
        norm2_bias,
    )
    passage = tower(passage_tokens, passage_cotangent, passage_segments, passage_cls, weights, 1)
    query = tower(query_tokens, query_cotangent, query_segments, query_cls, weights, 0)
    stacked = [
        jnp.stack([query_part, passage_part])
        for query_part, passage_part in zip(query[3], passage[3])
    ]
    layered = [
        jnp.stack([query_part, passage_part])
        for query_part, passage_part in zip(query[4], passage[4])
    ]
    big_grads = lax.psum(
        (
            stacked[0],
            stacked[1],
            stacked[2],
            stacked[3],
            stacked[4],
            stacked[5],
            stacked[6],
            stacked[7],
            stacked[8],
        ),
        "wide",
    )
    small_grads = lax.psum(
        (layered[0], layered[1], layered[2], layered[3], layered[4], layered[5]), ("wide", "narrow")
    )
    return (
        query[0],
        passage[0],
        query[1],
        passage[1],
        query[2],
        passage[2],
        big_grads[0],
        big_grads[1],
        big_grads[2],
        big_grads[3],
        big_grads[4],
        big_grads[5],
        small_grads[0],
        small_grads[1],
        small_grads[2],
        big_grads[6],
        big_grads[7],
        big_grads[8],
        small_grads[3],
        small_grads[4],
        small_grads[5],
    )


def solution(mesh):
    placed = (
        P(("wide", "narrow"), None),
        P(("wide", "narrow"), None),
        P(("wide", "narrow"), None),
        P(("wide", "narrow"), None),
        P("wide", None),
        P("wide", None),
        P("wide", None),
        P("wide", None),
        P(None, None, "narrow"),
        P(None, "narrow"),
        P(None, None, "narrow"),
        P(None, None, "narrow"),
        P(None, "narrow"),
        P(None, "narrow", None),
        P(),
        P(),
        P(),
        P(None, None, "narrow"),
        P(None, "narrow"),
        P(None, "narrow", None),
        P(),
        P(),
        P(),
    )
    return jax.shard_map(
        per_device,
        mesh=mesh,
        in_specs=placed,
        out_specs=(
            P(("wide", "narrow"), None),
            P(("wide", "narrow"), None),
            P(("wide", "narrow"), None),
            P(("wide", "narrow"), None),
            P("wide", None, "narrow"),
            P("wide", None, "narrow"),
            P(None, None, "narrow"),
            P(None, "narrow"),
            P(None, None, "narrow"),
            P(None, None, "narrow"),
            P(None, "narrow"),
            P(None, "narrow", None),
            P(),
            P(),
            P(),
            P(None, None, "narrow"),
            P(None, "narrow"),
            P(None, "narrow", None),
            P(),
            P(),
            P(),
        ),
        check_vma=False,
    )
```

profile of v0, /device:TPU:0, one launch (start us, length us, event | category | flops | bytes accessed | tf_op | source)
XLA Modules:
  0.0 994.1 jit_solution(7820239422888187306)
XLA Ops:
  9.5 1.8 slice_bitcast_fusion.8
  12.2 50.1 %all-gather.5.cloned.1.call-done = bf16[1536,768]{1,0:T(8,128)(2,1)} async-done(((bf16[384,768]{1,0:T(8,128)(2,1)}), bf16[1536,768]{1,0:T(8,128)(2,1)}) %all-gather.5.cloned.1.call-update) | async-done | bytes 2359312 | tf_op jit(solution)/shard_map/all_gather | solution.py:119
  62.3 3.2 convolution_bitcast_fusion
  67.7 12.4 %while.4 = (s32[]{:T(128)}, bf16[3,512,3,64]{1,3,2,0:T(8,128)(2,1)S(1)}, f32[3,3,512,1]{2,1,3,0:T(4,128)}, bf16[3,512,3,64]{1,3,2,0:T(8,128)(2,1)S(1)}, s32[3,51...) while((s32[]{:T(128)}, ...), condition=%wide.region_11.12_spmd, body=%wide.region_8.11_spmd.sunk | while | flops 211290112 | bytes 11545701 | solution.py:127
  81.6 3.0 fusion.134
  86.6 82.3 %reduce-scatter.19.cloned.1.call-done = f32[384,768]{1,0:T(8,128)} async-done(((f32[1536,768]{1,0:T(8,128)}), f32[384,768]{1,0:T(8,128)}) %reduce-scatter.19.cloned.1.call-update) | async-done | bytes 1179664 | tf_op jit(solution)/shard_map/reduce_scatter | solution.py:131
  168.9 1.5 fusion.165
  173.4 49.8 %all-gather.7.cloned.1.call-done = bf16[1536,768]{1,0:T(8,128)(2,1)} async-done(((bf16[384,768]{1,0:T(8,128)(2,1)}), bf16[1536,768]{1,0:T(8,128)(2,1)}) %all-gather.7.cloned.1.call-update) | async-done | bytes 2359312 | tf_op jit(solution)/shard_map/all_gather | solution.py:137
  223.2 14.0 %fusion.49 = (bf16[1536,768]{1,0:T(8,128)(2,1)S(1)}, f32[1536,768]{1,0:T(8,128)}) fusion(f32[768]{0:T(1024)S(1)} %get-tuple-element.242, bf16[1536,768]{1,0:T(8,128)(2,1)} %all-gather.7.cloned.1.call-done, bf16[2,768,768]{2,1,0:T(8,128)(2,1)S(1)} %copy-done.103), kind=kOutput, calls=%fused_computation.64 | convolution fusion | flops 1889796096 | bytes 10620928 | tf_op jit(solution)/shard_map/dot_general | solution.py:13
  237.2 1.4 copy-done.21
  238.6 4.3 fusion.95
  243.8 27.2 %all_gather.24 = bf16[512,768]{1,0:T(8,128)(2,1)S(1)} all-gather(bf16[128,768]{1,0:T(8,128)(2,1)S(1)} %copy-done.43), channel_id=1, replica_groups=mesh['wide'=8,'narrow'=4] {'narrow'}, dimensions={0}, use_global_device_ids=true | all-gather | bytes 983040 | tf_op jit(solution)/shard_map/all_gather | solution.py:119
  276.3 1.6 fusion.137
  279.2 57.7 %reduce-scatter.21.cloned.1.call-done = f32[384,768]{1,0:T(8,128)} async-done(((f32[1536,768]{1,0:T(8,128)}), f32[384,768]{1,0:T(8,128)}) %reduce-scatter.21.cloned.1.call-update) | async-done | bytes 1179664 | tf_op jit(solution)/shard_map/reduce_scatter | solution.py:140
  337.0 2.1 fusion.164
  340.6 1.9 fusion.160
  344.5 31.1 %reduce-scatter.15.cloned.1.call-done = f32[128,768]{1,0:T(8,128)} async-done(((f32[512,768]{1,0:T(8,128)}), f32[128,768]{1,0:T(8,128)}) %reduce-scatter.15.cloned.1.call-update) | async-done | bytes 393232 | tf_op jit(solution)/shard_map/reduce_scatter | solution.py:131
  375.5 1.3 fusion.167
  377.9 24.8 %all_gather.25 = bf16[512,768]{1,0:T(8,128)(2,1)S(1)} all-gather(bf16[128,768]{1,0:T(8,128)(2,1)S(1)} %fusion.132), channel_id=1, replica_groups=mesh['wide'=8,'narrow'=4] {'narrow'}, dimensions={0}, use_global_device_ids=true | all-gather | bytes 983040 | tf_op jit(solution)/shard_map/all_gather | solution.py:137
  402.7 6.2 fusion.70
  409.8 1.9 fusion.102
  411.8 21.3 %all-gather.9.cloned.1.call-done = bf16[1536,768]{1,0:T(8,128)(2,1)} async-done(((bf16[384,768]{1,0:T(8,128)(2,1)}), bf16[1536,768]{1,0:T(8,128)(2,1)}) %all-gather.9.cloned.1.call-update) | async-done | bytes 2359312 | tf_op jit(solution)/shard_map/all_gather | solution.py:157
  433.1 7.6 convert_reduce_fusion
  440.7 1.4 copy-done.24
  442.1 4.3 fusion.97
  446.4 23.7 %reduce-scatter.17.cloned.1.call-done = f32[128,768]{1,0:T(8,128)} async-done(((f32[512,768]{1,0:T(8,128)}), f32[128,768]{1,0:T(8,128)}) %reduce-scatter.17.cloned.1.call-update) | async-done | bytes 393232 | tf_op jit(solution)/shard_map/reduce_scatter | solution.py:140
  470.2 1.4 fusion.166
  471.8 1.9 fusion.129
  473.7 2.2 fusion.158
  476.6 29.4 %all_gather.28 = bf16[512,768]{1,0:T(8,128)(2,1)S(1)} all-gather(bf16[128,768]{1,0:T(8,128)(2,1)S(1)} %convert_element_type.178), channel_id=1, replica_groups=mesh['wide'=8,'narrow'=4] {'narrow'}, dimensions={0}, use_global_device_ids=true | all-gather | bytes 983040 | tf_op jit(solution)/shard_map/all_gather | solution.py:157
  506.0 1.7 convert_reduce_fusion.2
  508.6 2.1 fusion.104
  510.8 58.7 %reduce-scatter.27.cloned.1.call-done = f32[384,768]{1,0:T(8,128)} async-done(((f32[1536,768]{1,0:T(8,128)}), f32[384,768]{1,0:T(8,128)}) %reduce-scatter.27.cloned.1.call-update) | async-done | bytes 1179664 | tf_op jit(solution)/shard_map/reduce_scatter | solution.py:164
  569.4 3.3 multiply_reduce_fusion.2
  575.7 1.7 fusion.113
  577.5 1.7 copy.105
  579.2 1.7 copy.115
  581.0 27.0 %reduce-scatter.23.cloned.1.call-done = f32[128,768]{1,0:T(8,128)} async-done(((f32[512,768]{1,0:T(8,128)}), f32[128,768]{1,0:T(8,128)}) %reduce-scatter.23.cloned.1.call-update) | async-done | bytes 393232 | tf_op jit(solution)/shard_map/reduce_scatter | solution.py:164
  608.0 1.4 multiply_reduce_fusion.7
  611.1 25.1 %all_gather.29 = bf16[512,768]{1,0:T(8,128)(2,1)S(1)} all-gather(bf16[128,768]{1,0:T(8,128)(2,1)S(1)} %convert_element_type.180), channel_id=1, replica_groups=mesh['wide'=8,'narrow'=4] {'narrow'}, dimensions={0}, use_global_device_ids=true | all-gather | bytes 983040 | tf_op jit(solution)/shard_map/all_gather | solution.py:173
  638.5 1.2 multiply_reduce_fusion.1
  642.6 1.7 convolution_convert_fusion.2
  646.6 19.5 %all-gather.11.cloned.1.call-done = bf16[1536,768]{1,0:T(8,128)(2,1)} async-done(((bf16[384,768]{1,0:T(8,128)(2,1)}), bf16[1536,768]{1,0:T(8,128)(2,1)}) %all-gather.11.cloned.1.call-update) | async-done | bytes 2359312 | tf_op jit(solution)/shard_map/all_gather | solution.py:173
  666.1 2.6 convolution_convert_fusion.1
  670.3 20.4 %while.5 = (s32[]{:T(128)}, bf16[3,512,3,64]{1,3,2,0:T(8,128)(2,1)S(1)}, bf16[3,512,3,64]{1,3,2,0:T(8,128)(2,1)S(1)}, bf16[3,512,3,64]{1,3,2,0:T(8,128)(2,1)S(1)...) while((s32[]{:T(128)}, ...), condition=%wide.region_32.33_spmd, body=%wide.region_30.32_spmd.sunk | while | flops 511114240 | bytes 26718332 | solution.py:176
  672.0 1.5 fusion.240
  678.8 1.6 fusion.240
  685.7 1.5 fusion.240
  694.4 3.6 convolution_convert_fusion
  704.7 2.1 convolution_bitcast_fusion.3
  706.8 2.7 pad_maximum_fusion
  709.5 1.4 copy-done.23
  710.9 2.0 convolution_bitcast_fusion.1
  713.0 2.5 pad_maximum_fusion.1
  719.0 1.5 convolution_bitcast_fusion.5
  726.5 1.6 add_convert_fusion.2
  728.3 4.0 reduce-scatter.33.cloned.1.call-done
  734.1 43.5 %all-reduce = (f32[2,768]{1,0:T(2,128)}, f32[2,768]{1,0:T(2,128)}, f32[2,768]{1,0:T(2,128)}, f32[2,768]{1,0:T(2,128)}, f32[2,768]{1,0:T(2,128)}, /*index=5*/f32[2,768]{1,0:T(2,128)}) all-reduce(f32[2,768]{1,0:T(2,128)S(1)} %pad_maximum_fusion.15, ...), channel_id=1, replica_groups=mesh['wide'=8,'narrow'=4] {'wide','narrow'}, use_global_device_ids=true, to_apply=%region_48.49 | all-reduce | flops 9216 | bytes 73728 | tf_op jit(solution)/shard_map/psum | solution.py:281
  778.0 23.7 %all-reduce.1 = (f32[2,192]{1,0:T(2,128)}, f32[2,192]{1,0:T(2,128)}, f32[2,768]{1,0:T(2,128)}) all-reduce(f32[2,192]{1,0:T(2,128)S(1)} %pad_maximum_fusion.22, f32[2,192]{1,0:T(2,128)S(1)} %pad_maximum_fusion.23, f32[2,768]{1,0:T(2,128)S(1)} %pad_maximum_fusion.18), channel_id=1, replica_groups=mesh['wide'=8,'narrow'=4] {'wide'}, use_global_device_ids=true, to_apply=%region_39.40 | all-reduce | flops 2304 | bytes 18432 | tf_op jit(solution)/shard_map/psum | solution.py:267
  801.7 2.0 add_convert_fusion
  803.7 172.8 %all-reduce.5.cloned.1.call-done = (f32[2,768,192]{1,2,0:T(8,128)}, f32[2,768,192]{1,2,0:T(8,128)}, f32[2,768,192]{1,2,0:T(8,128)}, f32[2,192,768]{2,1,0:T(8,128...) async-done(((f32[2,768,192]{1,2,0:T(8,128)}, f32[2,768,192]{1,2,0:T(8,128)}, f32[2,768,192]{1,2,0:T(8,128)}, f32[2,192,768]{2,1,0:T(8,128)}, f32[2,768,768]{2,1,0:T(8,128)}, ...) | async-done | bytes 14155792 | tf_op jit(solution)/shard_map/psum | solution.py:267
  976.5 2.5 copy.152
  982.6 2.2 copy.156
  985.1 2.2 copy.157
  (439 shorter events, 93.3 us)
Async XLA Ops:
  7.2 4.2 copy-start.54
  7.2 4.2 copy-start.55
  7.2 55.1 %all-gather.5.cloned.1.call-start = ((), (), s32[]{:S(2)}) async-start(), calls=%async_computation.12 | async-start | bytes 2949120 | tf_op jit(solution)/shard_map/all_gather | solution.py:119
  7.9 161.0 %reduce-scatter.19.cloned.1.call-start = ((), (), s32[]{:S(2)}) async-start(), calls=%async_computation.13 | async-start | bytes 5898240 | tf_op jit(solution)/shard_map/reduce_scatter | solution.py:131
  11.4 51.0 %copy-start.64 = (bf16[768,192]{0,1:T(8,128)(2,1)}, bf16[768,192]{0,1:T(8,128)(2,1)S(1)}, u32[]{:S(2)}) copy-start(bf16[768,192]{0,1:T(8,128)(2,1)S(1)} %get-tuple-element.336) | copy-start | bytes 884740
  12.2 53.4 %copy-start.56 = (bf16[768,192]{0,1:T(8,128)(2,1)}, bf16[768,192]{0,1:T(8,128)(2,1)S(1)}, u32[]{:S(2)}) copy-start(bf16[768,192]{0,1:T(8,128)(2,1)S(1)} %get-tuple-element.340) | copy-start | bytes 884740
  12.2 53.4 %copy-start.58 = (bf16[768,192]{0,1:T(8,128)(2,1)}, bf16[768,192]{0,1:T(8,128)(2,1)S(1)}, u32[]{:S(2)}) copy-start(bf16[768,192]{0,1:T(8,128)(2,1)S(1)} %get-tuple-element.362) | copy-start | bytes 884740
  12.2 258.9 %copy-start.60 = (bf16[768,192]{0,1:T(8,128)(2,1)}, bf16[768,192]{0,1:T(8,128)(2,1)S(1)}, u32[]{:S(2)}) copy-start(bf16[768,192]{0,1:T(8,128)(2,1)S(1)} %get-tuple-element.341) | copy-start | bytes 884740
  80.1 4.5 copy-start.2
  80.1 4.5 copy-start.4
  80.1 4.5 copy-start.14
  84.7 84.2 %copy-start.26 = (bf16[384,768]{1,0:T(8,128)(2,1)S(1)}, bf16[384,768]{1,0:T(8,128)(2,1)}, u32[]{:S(2)}) copy-start(bf16[384,768]{1,0:T(8,128)(2,1)} %param.28) | copy-start | bytes 1769476
  84.7 138.5 %all-gather.7.cloned.1.call-start = ((), (), s32[]{:S(2)}) async-start(), calls=%async_computation.14 | async-start | bytes 2949120 | tf_op jit(solution)/shard_map/all_gather | solution.py:137
  170.4 52.7 %copy-start.103 = (bf16[2,768,768]{2,1,0:T(8,128)(2,1)S(1)}, bf16[2,768,768]{2,1,0:T(8,128)(2,1)}, u32[]{:S(2)}) copy-start(bf16[2,768,768]{2,1,0:T(8,128)(2,1)} %param.44) | copy-start | bytes 7077892
  172.5 164.5 %reduce-scatter.21.cloned.1.call-start = ((), (), s32[]{:S(2)}) async-start(), calls=%async_computation.15 | async-start | bytes 5898240 | tf_op jit(solution)/shard_map/reduce_scatter | solution.py:140
  173.4 63.8 %copy-start.95 = (f32[768]{0:T(1024)}, f32[768]{0:T(1024)S(1)}, u32[]{:S(2)}) copy-start(f32[768]{0:T(1024)S(1)} %get-tuple-element.242) | copy-start | bytes 9220
  223.2 15.5 %copy-start.100 = (bf16[2,768,768]{2,1,0:T(8,128)(2,1)S(1)}, bf16[2,768,768]{2,1,0:T(8,128)(2,1)}, u32[]{:S(2)}) copy-start(bf16[2,768,768]{2,1,0:T(8,128)(2,1)} %param.46) | copy-start | bytes 7077892
  242.9 28.2 %copy-start.62 = (bf16[768,192]{0,1:T(8,128)(2,1)S(1)}, bf16[768,192]{0,1:T(8,128)(2,1)}, u32[]{:S(2)}) copy-start(bf16[768,192]{0,1:T(8,128)(2,1)} %get-tuple-element.361) | copy-start | bytes 884740
  242.9 28.2 %copy-start.66 = (bf16[768,192]{0,1:T(8,128)(2,1)S(1)}, bf16[768,192]{0,1:T(8,128)(2,1)}, u32[]{:S(2)}) copy-start(bf16[768,192]{0,1:T(8,128)(2,1)} %get-tuple-element.337) | copy-start | bytes 884740
  242.9 132.6 %reduce-scatter.15.cloned.1.call-start = ((), (), s32[]{:S(2)}) async-start(), calls=%async_computation.10 | async-start | bytes 1966080 | tf_op jit(solution)/shard_map/reduce_scatter | solution.py:131
  277.9 155.2 %all-gather.9.cloned.1.call-start = ((), (), s32[]{:S(2)}) async-start(), calls=%async_computation.18 | async-start | bytes 2949120 | tf_op jit(solution)/shard_map/all_gather | solution.py:157
  344.4 125.8 %reduce-scatter.17.cloned.1.call-start = ((), (), s32[]{:S(2)}) async-start(), calls=%async_computation.11 | async-start | bytes 1966080 | tf_op jit(solution)/shard_map/reduce_scatter | solution.py:140
  375.5 27.2 %copy-start.104 = (bf16[2,768,768]{2,1,0:T(8,128)(2,1)S(1)}, bf16[2,768,768]{2,1,0:T(8,128)(2,1)}, u32[]{:S(2)}) copy-start(bf16[2,768,768]{2,1,0:T(8,128)(2,1)} %param.44) | copy-start | bytes 7077892
  376.9 25.9 %copy-start.85 = (f32[128]{0:T(128)}, f32[128]{0:T(128)S(1)}, u32[]{:S(2)}) copy-start(f32[128]{0:T(128)S(1)} %broadcast_multiply_fusion.11) | copy-start | bytes 1540
  377.1 25.6 %copy-start.87 = (f32[128]{0:T(128)}, f32[128]{0:T(128)S(1)}, u32[]{:S(2)}) copy-start(f32[128]{0:T(128)S(1)} %add_rsqrt_fusion.3) | copy-start | bytes 1540
  402.7 6.2 copy-start.39
  402.7 7.1 copy-start.101
  411.8 157.6 %reduce-scatter.27.cloned.1.call-start = ((), (), s32[]{:S(2)}) async-start(), calls=%async_computation.19 | async-start | bytes 5898240 | tf_op jit(solution)/shard_map/reduce_scatter | solution.py:164
  433.1 9.0 copy-start.105
  446.4 161.5 %reduce-scatter.23.cloned.1.call-start = ((), (), s32[]{:S(2)}) async-start(), calls=%async_computation.16 | async-start | bytes 1966080 | tf_op jit(solution)/shard_map/reduce_scatter | solution.py:164
  470.2 3.5 copy-start.36
  470.2 35.9 %copy-start.113 = (f32[512,768]{1,0:T(8,128)S(1)}, f32[512,768]{1,0:T(8,128)}, u32[]{:S(2)}) copy-start(f32[512,768]{1,0:T(8,128)} %get-tuple-element.352) | copy-start | bytes 4718596
  471.7 34.3 %copy-start.102 = (bf16[2,768,768]{2,1,0:T(8,128)(2,1)S(1)}, bf16[2,768,768]{2,1,0:T(8,128)(2,1)}, u32[]{:S(2)}) copy-start(bf16[2,768,768]{2,1,0:T(8,128)(2,1)} %param.46) | copy-start | bytes 7077892
  506.0 2.6 copy-start.106
  510.7 155.4 %all-gather.11.cloned.1.call-start = ((), (), s32[]{:S(2)}) async-start(), calls=%async_computation.20 | async-start | bytes 2949120 | tf_op jit(solution)/shard_map/all_gather | solution.py:173
  569.4 3.3 copy-start.1
  574.8 33.2 %copy-start.86 = (f32[128]{0:T(128)S(1)}, f32[128]{0:T(128)}, u32[]{:S(2)}) copy-start(f32[128]{0:T(128)} %copy-done.85) | copy-start | bytes 1540
  575.7 149.0 %reduce-scatter.31.cloned.1.call-start = ((), (), s32[]{:S(2)}) async-start(), calls=%async_computation.22 | async-start | bytes 245760
  580.9 145.6 %reduce-scatter.25.cloned.1.call-start = ((), (), s32[]{:S(2)}) async-start(), calls=%async_computation.17 | async-start | bytes 983040 | tf_op jit(solution)/shard_map/reduce_scatter | solution.py:192
  609.3 27.7 %copy-start.52 = (bf16[2,192,768]{2,1,0:T(8,128)(2,1)S(1)}, bf16[2,192,768]{2,1,0:T(8,128)(2,1)}, u32[]{:S(2)}) copy-start(bf16[2,192,768]{2,1,0:T(8,128)(2,1)} %param.40) | copy-start | bytes 1769476
  609.4 28.1 %copy-start.10 = (pred[512,512]{0,1:T(8,128)(4,1)S(1)}, pred[512,512]{0,1:T(8,128)(4,1)}, u32[]{:S(2)}) copy-start(pred[512,512]{0,1:T(8,128)(4,1)} %copy-done.9) | copy-start | bytes 786436
  609.4 28.1 %copy-start.74 = (f32[3,512]{1,0:T(4,128)S(1)}, f32[3,512]{1,0:T(4,128)}, u32[]{:S(2)}) copy-start(f32[3,512]{1,0:T(4,128)} %get-tuple-element.343) | copy-start | bytes 18436
  638.4 3.5 copy-start.68
  644.3 21.7 %copy-start.53 = (bf16[2,192,768]{2,1,0:T(8,128)(2,1)S(1)}, bf16[2,192,768]{2,1,0:T(8,128)(2,1)}, u32[]{:S(2)}) copy-start(bf16[2,192,768]{2,1,0:T(8,128)(2,1)} %param.40) | copy-start | bytes 1769476
  644.4 87.9 %reduce-scatter.33.cloned.1.call-start = ((), (), s32[]{:S(2)}) async-start(), calls=%async_computation.23 | async-start | bytes 245760
  646.5 155.1 %reduce-scatter.29.cloned.1.call-start = ((), (), s32[]{:S(2)}) async-start(), calls=%async_computation.21 | async-start | bytes 2949120 | tf_op jit(solution)/shard_map/reduce_scatter | solution.py:192
  698.0 278.5 %all-reduce.5.cloned.1.call-start = ((), (), s32[]{:S(2)}) async-start(), calls=%async_computation.24 | async-start | bytes 28311552 | tf_op jit(solution)/shard_map/psum | solution.py:267
  706.8 2.7 copy-start.22
  706.8 4.1 copy-start.23
  712.9 2.6 copy-start.12
  712.9 3.2 copy-start.108
  723.9 2.6 copy-start.16
  723.9 4.2 copy-start.77
  723.9 4.2 copy-start.76
  724.0 4.2 copy-start.82
  724.0 10.0 %copy-start.96 = (f32[768]{0:T(1024)S(1)}, f32[768]{0:T(1024)}, u32[]{:S(2)}) copy-start(f32[768]{0:T(1024)} %get-tuple-element.357) | copy-start | bytes 9220
  724.0 10.0 %copy-start.84 = (f32[768]{0:T(1024)S(1)}, f32[768]{0:T(1024)}, u32[]{:S(2)}) copy-start(f32[768]{0:T(1024)} %get-tuple-element.220) | copy-start | bytes 9220
  724.0 10.0 %copy-start.78 = (f32[768]{0:T(1024)S(1)}, f32[768]{0:T(1024)}, u32[]{:S(2)}) copy-start(f32[768]{0:T(1024)} %get-tuple-element.309) | copy-start | bytes 9220
  724.0 10.0 %copy-start.83 = (f32[768]{0:T(1024)S(1)}, f32[768]{0:T(1024)}, u32[]{:S(2)}) copy-start(f32[768]{0:T(1024)} %get-tuple-element.225) | copy-start | bytes 9220
  724.0 77.7 %copy-start.7 = (f32[384,768]{1,0:T(8,128)S(1)}, f32[384,768]{1,0:T(8,128)}, u32[]{:S(2)}) copy-start(f32[384,768]{1,0:T(8,128)} %copy-done.6) | copy-start | bytes 3538948
  976.5 3.5 copy-start.34
  976.5 4.5 copy-start.33
  979.0 3.6 copy-start.13
  981.1 3.8 slice-start
  (67 other events, 93.2 us)
Sparse Core Ops, SparseCore 0:
  9.6 52.6 all-gather.4
  84.8 84.0 reduce-scatter.18
  172.6 50.4 all-gather.6
  243.1 93.8 reduce-scatter.20
  339.1 36.3 reduce-scatter.14
  377.5 55.5 all-gather.8
  435.4 34.6 reduce-scatter.16
  473.0 96.3 reduce-scatter.26
  571.7 36.1 reduce-scatter.22
  609.9 56.0 all-gather.10
  668.3 18.8 reduce-scatter.30
  689.4 21.4 reduce-scatter.24
  713.1 19.1 reduce-scatter.32
  734.4 46.9 reduce-scatter.28
  787.7 188.7 all-reduce.4
where the time goes:
time: 1000 us; the launch traced here: 994 us
  waiting for transfers between devices  599 us (60%)
  blocking collectives  174 us (17%)
  matrix products  92.8 us (9%)
  local copies, waits for them, and re-layouts  58 us (6%)
  other arithmetic  53.8 us (5%)
  between operations  15.6 us (2%)
    psum x1, waiting for transfers between devices, per_device(): lax.psum((stacked[0], stacked[1], stacked[2], stacked[3], stacked[4], sta...  173 us
    reduce_scatter x2, waiting for transfers between devices, tower(): lax.psum_scatter(matmul(attended, out_weight), 'narrow', scatter_dimensio...  113 us
    reduce_scatter x2, waiting for transfers between devices, tower(): lax.psum_scatter(matmul_right(grad_inner, inner_weight), 'narrow', scatte...  85.6 us
    reduce_scatter x2, waiting for transfers between devices, tower(): lax.psum_scatter(matmul(activated, outer_weight), 'narrow', scatter_dimen...  81.5 us
    all_gather x1, waiting for transfers between devices, tower(): full_rows = lax.all_gather(tokens, 'narrow', axis=0, tiled=True)  50.1 us
    all_gather x1, waiting for transfers between devices, tower(): lax.all_gather(hidden1.astype(jnp.bfloat16), 'narrow', axis=0, tiled=True)  49.8 us
    unnamed x252, local copies, waits for them, and re-layouts  43.6 us
    psum x1, blocking collectives, per_device(): lax.psum((layered[0], layered[1], layered[2], layered[3], layered[4], lay...  43.5 us
  transfers between devices with their start and end apart: 15, of which 12 were waited for; matrix products, arithmetic and copies ran while one was open for 13% of the time, Pallas kernels for 0%

commit v1 on v0

--- a/solution.py
+++ b/solution.py
@@ -7,6 +7,27 @@
 HDIM = 64
 NORM_EPS = 1e-05
 MASKED = -1e30
+
+
+def clear_goods_on_mesh(sheet, shard_axis, out_dim):
+    last = lax.psum(1, shard_axis)
+    field_out = lax.axis_index(shard_axis)
+    low, x_new, r1 = (last, field_out, sheet.shape[out_dim])
+    buffers = [(c, (c + 1) % low) for c in range(low)]
+    store = [(c, (c - 1) % low) for c in range(low)]
+    u1 = jnp.zeros((*sheet.shape[:out_dim], low * r1, *sheet.shape[out_dim + 1 :]), sheet.dtype)
+    u1 = lax.dynamic_update_slice_in_dim(u1, sheet, x_new * r1, axis=out_dim)
+    y_new = low // 2
+    found_now = latest = sheet
+    j0 = 1
+    while j0 < y_new + 1:
+        found_now = lax.ppermute(found_now, shard_axis, buffers)
+        u1 = lax.dynamic_update_slice_in_dim(u1, found_now, (x_new - j0) % low * r1, axis=out_dim)
+        if j0 < low - y_new:
+            latest = lax.ppermute(latest, shard_axis, store)
+            u1 = lax.dynamic_update_slice_in_dim(u1, latest, (x_new + j0) % low * r1, axis=out_dim)
+        j0 += 1
+    return u1
 
 
 def matmul(left, right):
@@ -170,7 +191,7 @@
     grad_bias1 = jnp.sum(grad_hidden1, 0)
     grad_resid1 = norm_back(grad_hidden1, normed1, inverse1, norm1_gain)
     grad_out_bias = jnp.sum(grad_resid1, 0)
-    resid1_full = lax.all_gather(grad_resid1.astype(jnp.bfloat16), "narrow", axis=0, tiled=True)
+    resid1_full = clear_goods_on_mesh(grad_resid1.astype(jnp.bfloat16), "narrow", out_dim=0)
     grad_out_weight = matmul_left(attended, resid1_full)
     grad_attended = matmul_right(resid1_full, out_weight).astype(jnp.bfloat16).reshape(split_shape)
     grad_query, grad_key, grad_value = lax.map(

time: 1000 us -> 966 us (0.966)
  waiting for transfers between devices: 599 us -> 557 us
  blocking collectives: 174 us -> 146 us
  local copies, waits for them, and re-layouts: 58 us -> 75.4 us
  starting transfers between devices: 1.01 us -> 11.7 us
    ppermute x0 -> x6, waiting for transfers between devices: none -> 54.4 us  [the longest x4 44.7 us: clear_goods_on_mesh(): found_now = lax.ppermute(found_now, shard_axis, buffers)]
    psum x1, waiting for transfers between devices: 173 us -> 142 us  [per_device(): lax.psum((stacked[0], stacked[1], stacked[2], stacked[3], stacked[4], sta...]
    all_gather x1, waiting for transfers between devices: 49.8 us -> 24.2 us  [tower(): lax.all_gather(hidden1.astype(jnp.bfloat16), 'narrow', axis=0, tiled=True)]
    all_gather x1 -> x0, blocking collectives: 25.1 us -> none  [tower(): lax.all_gather(grad_resid1.astype(jnp.bfloat16), 'narrow', axis=0, tiled=...]
    all_gather x1 -> x0, waiting for transfers between devices: 19.5 us -> none  [tower(): lax.all_gather(grad_resid1.astype(jnp.bfloat16), 'narrow', axis=0, tiled=...]
    reduce_scatter x2, waiting for transfers between devices: 113 us -> 99.5 us  [tower(): lax.psum_scatter(matmul(attended, out_weight), 'narrow', scatter_dimensio...]
    ppermute x0 -> x6, starting transfers between devices: none -> 10.4 us  [the longest x2 5.78 us: clear_goods_on_mesh(): latest = lax.ppermute(latest, shard_axis, store)]
    unnamed x252 -> x248, local copies, waits for them, and re-layouts: 43.6 us -> 37.9 us
  transfers between devices with their start and end apart: 15 -> 20, of which waited for: 12 -> 16; matrix products, arithmetic and copies ran while one was open for 13% -> 17% of each run, Pallas kernels for 0% -> 0%
where the time goes in v1:
time: 966 us; the launch traced here: 956 us
  waiting for transfers between devices  557 us (58%)
  blocking collectives  146 us (15%)
  matrix products  95.9 us (10%)
  local copies, waits for them, and re-layouts  75.4 us (8%)
  other arithmetic  54.2 us (6%)
  between operations  15.6 us (2%)
  starting transfers between devices  11.7 us (1%)
    psum x1, waiting for transfers between devices, per_device(): lax.psum((stacked[0], stacked[1], stacked[2], stacked[3], stacked[4], sta...  142 us
    reduce_scatter x2, waiting for transfers between devices, tower(): lax.psum_scatter(matmul(attended, out_weight), 'narrow', scatter_dimensio...  99.5 us
    reduce_scatter x2, waiting for transfers between devices, tower(): lax.psum_scatter(matmul(activated, outer_weight), 'narrow', scatter_dimen...  86.4 us
    reduce_scatter x2, waiting for transfers between devices, tower(): lax.psum_scatter(matmul_right(grad_inner, inner_weight), 'narrow', scatte...  77.6 us
    all_gather x1, waiting for transfers between devices, tower(): full_rows = lax.all_gather(tokens, 'narrow', axis=0, tiled=True)  50.2 us
    ppermute x4, waiting for transfers between devices, clear_goods_on_mesh(): found_now = lax.ppermute(found_now, shard_axis, buffers)  44.7 us
    psum x1, blocking collectives, per_device(): lax.psum((layered[0], layered[1], layered[2], layered[3], layered[4], lay...  43.3 us
    unnamed x248, local copies, waits for them, and re-layouts  37.9 us
  transfers between devices with their start and end apart: 20, of which 16 were waited for; matrix products, arithmetic and copies ran while one was open for 17% of the time, Pallas kernels for 0%

profile of v1, /device:TPU:0, one launch (start us, length us, event | category | flops | bytes accessed | tf_op | source)
XLA Modules:
  0.0 956.2 jit_solution(4858402782248060281)
XLA Ops:
  9.5 1.8 slice_bitcast_fusion.8
  12.2 50.2 %all-gather.4.cloned.1.call-done = bf16[1536,768]{1,0:T(8,128)(2,1)} async-done(((bf16[384,768]{1,0:T(8,128)(2,1)}), bf16[1536,768]{1,0:T(8,128)(2,1)}) %all-gather.4.cloned.1.call-update) | async-done | bytes 2359312 | tf_op jit(solution)/shard_map/all_gather | solution.py:140
  62.3 3.2 convolution_bitcast_fusion
  67.7 12.4 %while.4 = (s32[]{:T(128)}, bf16[3,512,3,64]{1,3,2,0:T(8,128)(2,1)S(1)}, f32[3,3,512,1]{2,1,3,0:T(4,128)}, bf16[3,512,3,64]{1,3,2,0:T(8,128)(2,1)S(1)}, s32[3,51...) while((s32[]{:T(128)}, ...), condition=%wide.region_11.12_spmd, body=%wide.region_8.11_spmd.sunk | while | flops 211290112 | bytes 11545701 | solution.py:148
  81.6 3.0 fusion.134
  86.6 82.3 %reduce-scatter.19.cloned.1.call-done = f32[384,768]{1,0:T(8,128)} async-done(((f32[1536,768]{1,0:T(8,128)}), f32[384,768]{1,0:T(8,128)}) %reduce-scatter.19.cloned.1.call-update) | async-done | bytes 1179664 | tf_op jit(solution)/shard_map/reduce_scatter | solution.py:152
  172.6 24.0 %all_gather.18 = bf16[512,768]{1,0:T(8,128)(2,1)S(1)} all-gather(bf16[128,768]{1,0:T(8,128)(2,1)S(1)} %copy-done.48), channel_id=1, replica_groups=mesh['wide'=8,'narrow'=4] {'narrow'}, dimensions={0}, use_global_device_ids=true | all-gather | bytes 983040 | tf_op jit(solution)/shard_map/all_gather | solution.py:140
  204.3 24.2 %all-gather.6.cloned.1.call-done = bf16[1536,768]{1,0:T(8,128)(2,1)} async-done(((bf16[384,768]{1,0:T(8,128)(2,1)}), bf16[1536,768]{1,0:T(8,128)(2,1)}) %all-gather.6.cloned.1.call-update) | async-done | bytes 2359312 | tf_op jit(solution)/shard_map/all_gather | solution.py:158
  228.5 14.4 %fusion.49 = (bf16[1536,768]{1,0:T(8,128)(2,1)S(1)}, f32[1536,768]{1,0:T(8,128)}) fusion(f32[768]{0:T(1024)S(1)} %get-tuple-element.242, bf16[1536,768]{1,0:T(8,128)(2,1)} %all-gather.6.cloned.1.call-done, bf16[2,768,768]{2,1,0:T(8,128)(2,1)} %param.44), kind=kOutput, calls=%fused_computation.64 | convolution fusion | flops 1889796096 | bytes 10619904 | tf_op jit(solution)/shard_map/dot_general | solution.py:34
  244.3 4.3 fusion.95
  248.7 17.2 %reduce-scatter.15.cloned.1.call-done = f32[128,768]{1,0:T(8,128)} async-done(((f32[512,768]{1,0:T(8,128)}), f32[128,768]{1,0:T(8,128)}) %reduce-scatter.15.cloned.1.call-update) | async-done | bytes 393232 | tf_op jit(solution)/shard_map/reduce_scatter | solution.py:152
  268.3 25.8 %all_gather.19 = bf16[512,768]{1,0:T(8,128)(2,1)S(1)} all-gather(bf16[128,768]{1,0:T(8,128)(2,1)S(1)} %fusion.132), channel_id=1, replica_groups=mesh['wide'=8,'narrow'=4] {'narrow'}, dimensions={0}, use_global_device_ids=true | all-gather | bytes 983040 | tf_op jit(solution)/shard_map/all_gather | solution.py:158
  294.1 6.2 fusion.70
  301.2 1.9 fusion.102
  305.9 55.5 %reduce-scatter.21.cloned.1.call-done = f32[384,768]{1,0:T(8,128)} async-done(((f32[1536,768]{1,0:T(8,128)}), f32[384,768]{1,0:T(8,128)}) %reduce-scatter.21.cloned.1.call-update) | async-done | bytes 1179664 | tf_op jit(solution)/shard_map/reduce_scatter | solution.py:161
  361.4 2.2 fusion.164
  365.1 1.9 fusion.160
  368.9 31.0 %reduce-scatter.17.cloned.1.call-done = f32[128,768]{1,0:T(8,128)} async-done(((f32[512,768]{1,0:T(8,128)}), f32[128,768]{1,0:T(8,128)}) %reduce-scatter.17.cloned.1.call-update) | async-done | bytes 393232 | tf_op jit(solution)/shard_map/reduce_scatter | solution.py:161
  401.5 1.9 fusion.129
  403.4 2.2 fusion.158
  406.4 28.5 %all_gather.22 = bf16[512,768]{1,0:T(8,128)(2,1)S(1)} all-gather(bf16[128,768]{1,0:T(8,128)(2,1)S(1)} %convert_element_type.178), channel_id=1, replica_groups=mesh['wide'=8,'narrow'=4] {'narrow'}, dimensions={0}, use_global_device_ids=true | all-gather | bytes 983040 | tf_op jit(solution)/shard_map/all_gather | solution.py:178
  434.9 1.7 convert_reduce_fusion.2
  437.5 2.0 fusion.104
  439.6 21.4 %all-gather.8.cloned.1.call-done = bf16[1536,768]{1,0:T(8,128)(2,1)} async-done(((bf16[384,768]{1,0:T(8,128)(2,1)}), bf16[1536,768]{1,0:T(8,128)(2,1)}) %all-gather.8.cloned.1.call-update) | async-done | bytes 2359312 | tf_op jit(solution)/shard_map/all_gather | solution.py:178
  461.0 7.6 convert_reduce_fusion
  470.0 4.3 fusion.97
  474.4 24.1 %reduce-scatter.23.cloned.1.call-done = f32[128,768]{1,0:T(8,128)} async-done(((f32[512,768]{1,0:T(8,128)}), f32[128,768]{1,0:T(8,128)}) %reduce-scatter.23.cloned.1.call-update) | async-done | bytes 393232 | tf_op jit(solution)/shard_map/reduce_scatter | solution.py:185
  498.4 2.0 multiply_reduce_fusion.7
  504.4 3.7 collective-permute-start.1
  509.3 1.8 copy.115
  511.1 7.0 collective-permute-done
  518.1 2.8 collective-permute-start.2
  520.9 1.6 constant_dynamic-update-slice_fusion.9
  524.0 1.6 constant_dynamic-update-slice_fusion.8
  525.6 7.8 collective-permute-done.2
  540.8 1.7 convolution_convert_fusion.2
  543.0 53.6 %reduce-scatter.27.cloned.1.call-done = f32[384,768]{1,0:T(8,128)} async-done(((f32[1536,768]{1,0:T(8,128)}), f32[384,768]{1,0:T(8,128)}) %reduce-scatter.27.cloned.1.call-update) | async-done | bytes 1179664 | tf_op jit(solution)/shard_map/reduce_scatter | solution.py:185
  596.6 2.5 multiply_reduce_fusion.2
  599.5 1.7 broadcast_in_dim.137
  602.1 1.7 collective-permute-start.3
  603.8 2.1 collective-permute-start.4
  606.1 17.1 %collective-permute-done.3 = bf16[384,768]{1,0:T(8,128)(2,1)} collective-permute-done((bf16[384,768]{1,0:T(8,128)(2,1)S(1)}, bf16[384,768]{1,0:T(8,128)(2,1)}, u32[]{:S(2)}, u32[]{:S(2)}) %collective-permute-start.3) | collective-permute-done | bytes 589856 | tf_op jit(solution)/shard_map/ppermute | solution.py:24
  625.2 2.0 constant_dynamic-update-slice_fusion.5
  627.2 8.1 collective-permute-done.4
  635.3 1.9 constant_dynamic-update-slice_fusion.4
  637.2 12.9 %collective-permute-done.5 = bf16[384,768]{1,0:T(8,128)(2,1)} collective-permute-done((bf16[384,768]{1,0:T(8,128)(2,1)}, bf16[384,768]{1,0:T(8,128)(2,1)}, u32[]{:S(2)}, u32[]{:S(2)}) %collective-permute-start.5) | collective-permute-done | bytes 589856 | tf_op jit(solution)/shard_map/ppermute | solution.py:24
  650.1 2.0 constant_dynamic-update-slice_fusion.3
  652.1 2.6 convolution_convert_fusion.1
  659.1 26.9 %while.5 = (s32[]{:T(128)}, bf16[3,512,3,64]{1,3,2,0:T(8,128)(2,1)}, bf16[3,512,3,64]{1,3,2,0:T(8,128)(2,1)}, bf16[3,512,3,64]{1,3,2,0:T(8,128)(2,1)S(1)}, bf16[...) while((s32[]{:T(128)}, ...), condition=%wide.region_32.33_spmd, body=%wide.region_30.32_spmd.sunk | while | flops 511114240 | bytes 36155628 | solution.py:197
  689.8 3.5 convolution_convert_fusion
  693.5 2.2 convolution_bitcast_fusion.2
  699.9 2.1 convolution_bitcast_fusion.3
  702.0 2.7 pad_maximum_fusion
  706.1 2.1 convolution_bitcast_fusion.1
  708.2 2.5 pad_maximum_fusion.1
  710.7 2.5 convolution_bitcast_fusion.8
  722.6 1.6 add_convert_fusion.2
  726.2 43.3 %all-reduce = (f32[2,768]{1,0:T(2,128)}, f32[2,768]{1,0:T(2,128)}, f32[2,768]{1,0:T(2,128)}, f32[2,768]{1,0:T(2,128)}, f32[2,768]{1,0:T(2,128)}, /*index=5*/f32[2,768]{1,0:T(2,128)}) all-reduce(f32[2,768]{1,0:T(2,128)S(1)} %pad_maximum_fusion.15, ...), channel_id=1, replica_groups=mesh['wide'=8,'narrow'=4] {'wide','narrow'}, use_global_device_ids=true, to_apply=%region_48.49 | all-reduce | flops 9216 | bytes 73728 | tf_op jit(solution)/shard_map/psum | solution.py:302
  769.8 24.8 %all-reduce.1 = (f32[2,192]{1,0:T(2,128)}, f32[2,192]{1,0:T(2,128)}, f32[2,768]{1,0:T(2,128)}) all-reduce(f32[2,192]{1,0:T(2,128)S(1)} %pad_maximum_fusion.22, f32[2,192]{1,0:T(2,128)S(1)} %pad_maximum_fusion.23, f32[2,768]{1,0:T(2,128)S(1)} %pad_maximum_fusion.18), channel_id=1, replica_groups=mesh['wide'=8,'narrow'=4] {'wide'}, use_global_device_ids=true, to_apply=%region_39.40 | all-reduce | flops 2304 | bytes 18432 | tf_op jit(solution)/shard_map/psum | solution.py:288
  794.7 2.0 add_convert_fusion
  796.7 142.0 %all-reduce.5.cloned.1.call-done = (f32[2,768,192]{1,2,0:T(8,128)}, f32[2,768,192]{1,2,0:T(8,128)}, f32[2,768,192]{1,2,0:T(8,128)}, f32[2,192,768]{2,1,0:T(8,128...) async-done(((f32[2,768,192]{1,2,0:T(8,128)}, f32[2,768,192]{1,2,0:T(8,128)}, f32[2,768,192]{1,2,0:T(8,128)}, f32[2,192,768]{2,1,0:T(8,128)}, f32[2,768,768]{2,1,0:T(8,128)}, ...) | async-done | bytes 14155792 | tf_op jit(solution)/shard_map/psum | solution.py:288
  938.6 2.5 copy.159
  944.8 2.2 copy.163
  947.3 2.2 copy.164
  (475 shorter events, 121.6 us)
Async XLA Ops:
  7.2 4.1 copy-start.58
  7.2 4.1 copy-start.59
  7.2 55.1 %all-gather.4.cloned.1.call-start = ((), (), s32[]{:S(2)}) async-start(), calls=%async_computation.12 | async-start | bytes 2949120 | tf_op jit(solution)/shard_map/all_gather | solution.py:140
  7.9 160.9 %reduce-scatter.19.cloned.1.call-start = ((), (), s32[]{:S(2)}) async-start(), calls=%async_computation.13 | async-start | bytes 5898240 | tf_op jit(solution)/shard_map/reduce_scatter | solution.py:152
  11.3 51.0 %copy-start.68 = (bf16[768,192]{0,1:T(8,128)(2,1)}, bf16[768,192]{0,1:T(8,128)(2,1)S(1)}, u32[]{:S(2)}) copy-start(bf16[768,192]{0,1:T(8,128)(2,1)S(1)} %get-tuple-element.340) | copy-start | bytes 884740
  12.1 53.4 %copy-start.60 = (bf16[768,192]{0,1:T(8,128)(2,1)}, bf16[768,192]{0,1:T(8,128)(2,1)S(1)}, u32[]{:S(2)}) copy-start(bf16[768,192]{0,1:T(8,128)(2,1)S(1)} %get-tuple-element.344) | copy-start | bytes 884740
  12.2 53.4 %copy-start.62 = (bf16[768,192]{0,1:T(8,128)(2,1)}, bf16[768,192]{0,1:T(8,128)(2,1)S(1)}, u32[]{:S(2)}) copy-start(bf16[768,192]{0,1:T(8,128)(2,1)S(1)} %get-tuple-element.366) | copy-start | bytes 884740
  12.2 184.4 %copy-start.64 = (bf16[768,192]{0,1:T(8,128)(2,1)}, bf16[768,192]{0,1:T(8,128)(2,1)S(1)}, u32[]{:S(2)}) copy-start(bf16[768,192]{0,1:T(8,128)(2,1)S(1)} %get-tuple-element.345) | copy-start | bytes 884740
  80.1 4.5 copy-start.2
  80.1 4.5 copy-start.4
  80.1 4.5 copy-start.13
  84.7 84.2 %copy-start.25 = (bf16[384,768]{1,0:T(8,128)(2,1)S(1)}, bf16[384,768]{1,0:T(8,128)(2,1)}, u32[]{:S(2)}) copy-start(bf16[384,768]{1,0:T(8,128)(2,1)} %param.28) | copy-start | bytes 1769476
  84.7 143.8 %all-gather.6.cloned.1.call-start = ((), (), s32[]{:S(2)}) async-start(), calls=%async_computation.14 | async-start | bytes 2949120 | tf_op jit(solution)/shard_map/all_gather | solution.py:158
  86.6 84.2 %copy-start.79 = (f32[768]{0:T(1024)}, f32[768]{0:T(1024)S(1)}, u32[]{:S(2)}) copy-start(f32[768]{0:T(1024)S(1)} %get-tuple-element.246) | copy-start | bytes 9220
  170.7 25.9 %copy-start.66 = (bf16[768,192]{0,1:T(8,128)(2,1)S(1)}, bf16[768,192]{0,1:T(8,128)(2,1)}, u32[]{:S(2)}) copy-start(bf16[768,192]{0,1:T(8,128)(2,1)} %get-tuple-element.365) | copy-start | bytes 884740
  170.7 25.9 %copy-start.70 = (bf16[768,192]{0,1:T(8,128)(2,1)S(1)}, bf16[768,192]{0,1:T(8,128)(2,1)}, u32[]{:S(2)}) copy-start(bf16[768,192]{0,1:T(8,128)(2,1)} %get-tuple-element.341) | copy-start | bytes 884740
  172.5 93.4 %reduce-scatter.15.cloned.1.call-start = ((), (), s32[]{:S(2)}) async-start(), calls=%async_computation.10 | async-start | bytes 1966080 | tf_op jit(solution)/shard_map/reduce_scatter | solution.py:152
  203.5 157.9 %reduce-scatter.21.cloned.1.call-start = ((), (), s32[]{:S(2)}) async-start(), calls=%async_computation.15 | async-start | bytes 5898240 | tf_op jit(solution)/shard_map/reduce_scatter | solution.py:161
  204.3 38.5 %copy-start.100 = (f32[768]{0:T(1024)}, f32[768]{0:T(1024)S(1)}, u32[]{:S(2)}) copy-start(f32[768]{0:T(1024)S(1)} %get-tuple-element.242) | copy-start | bytes 9220
  228.5 15.8 %copy-start.105 = (bf16[2,768,768]{2,1,0:T(8,128)(2,1)S(1)}, bf16[2,768,768]{2,1,0:T(8,128)(2,1)}, u32[]{:S(2)}) copy-start(bf16[2,768,768]{2,1,0:T(8,128)(2,1)} %param.46) | copy-start | bytes 7077892
  248.6 151.3 %reduce-scatter.17.cloned.1.call-start = ((), (), s32[]{:S(2)}) async-start(), calls=%async_computation.11 | async-start | bytes 1966080 | tf_op jit(solution)/shard_map/reduce_scatter | solution.py:161
  265.9 28.2 %copy-start.108 = (bf16[2,768,768]{2,1,0:T(8,128)(2,1)S(1)}, bf16[2,768,768]{2,1,0:T(8,128)(2,1)}, u32[]{:S(2)}) copy-start(bf16[2,768,768]{2,1,0:T(8,128)(2,1)} %param.44) | copy-start | bytes 7077892
  267.2 26.9 %copy-start.94 = (f32[128]{0:T(128)}, f32[128]{0:T(128)S(1)}, u32[]{:S(2)}) copy-start(f32[128]{0:T(128)S(1)} %broadcast_multiply_fusion.11) | copy-start | bytes 1540
  267.4 26.6 %copy-start.95 = (f32[128]{0:T(128)}, f32[128]{0:T(128)S(1)}, u32[]{:S(2)}) copy-start(f32[128]{0:T(128)S(1)} %add_rsqrt_fusion.3) | copy-start | bytes 1540
  294.1 6.2 copy-start.45
  294.1 7.1 copy-start.106
  303.1 157.9 %all-gather.8.cloned.1.call-start = ((), (), s32[]{:S(2)}) async-start(), calls=%async_computation.18 | async-start | bytes 2949120 | tf_op jit(solution)/shard_map/all_gather | solution.py:178
  368.9 129.5 %reduce-scatter.23.cloned.1.call-start = ((), (), s32[]{:S(2)}) async-start(), calls=%async_computation.16 | async-start | bytes 1966080 | tf_op jit(solution)/shard_map/reduce_scatter | solution.py:185
  399.9 35.0 %copy-start.115 = (f32[512,768]{1,0:T(8,128)S(1)}, f32[512,768]{1,0:T(8,128)}, u32[]{:S(2)}) copy-start(f32[512,768]{1,0:T(8,128)} %get-tuple-element.356) | copy-start | bytes 4718596
  401.5 33.4 %copy-start.107 = (bf16[2,768,768]{2,1,0:T(8,128)(2,1)S(1)}, bf16[2,768,768]{2,1,0:T(8,128)(2,1)}, u32[]{:S(2)}) copy-start(bf16[2,768,768]{2,1,0:T(8,128)(2,1)} %param.46) | copy-start | bytes 7077892
  439.5 157.1 %reduce-scatter.27.cloned.1.call-start = ((), (), s32[]{:S(2)}) async-start(), calls=%async_computation.19 | async-start | bytes 5898240 | tf_op jit(solution)/shard_map/reduce_scatter | solution.py:185
  461.0 9.0 copy-start.110
  474.2 246.5 %reduce-scatter.31.cloned.1.call-start = ((), (), s32[]{:S(2)}) async-start(), calls=%async_computation.21 | async-start | bytes 245760
  500.4 7.7 copy-start.41
  500.4 7.7 copy-start.104
  504.2 13.9 %collective-permute-start = (bf16[128,768]{1,0:T(8,128)(2,1)}, bf16[128,768]{1,0:T(8,128)(2,1)}, u32[]{:S(2)}, u32[]{:S(2)}) collective-permute-start(bf16[128,768]{1,0:T(8,128)(2,1)} %get-tuple-element.315), channel_id=1, source_target_pairs={{0,1},{1,2},{2,3},{3,0},{4,5},{5,6},{6,7},{7,4},{8,9},{9,10},{10,1... | collective-permute-start | bytes 589832 | tf_op jit(solution)/shard_map/ppermute | solution.py:24
  504.4 19.6 %collective-permute-start.1 = (bf16[128,768]{1,0:T(8,128)(2,1)}, bf16[128,768]{1,0:T(8,128)(2,1)}, u32[]{:S(2)}, u32[]{:S(2)}) collective-permute-start(bf16[128,768]{1,0:T(8,128)(2,1)} %get-tuple-element.315), channel_id=1, source_target_pairs={{0,3},{1,0},{2,1},{3,2},{4,7},{5,4},{6,5},{7,6},{8,11},{9,8},{10,9... | collective-permute-start | bytes 589832 | tf_op jit(solution)/shard_map/ppermute | solution.py:27
  509.3 26.4 %copy-start.9 = (pred[512,512]{0,1:T(8,128)(4,1)S(1)}, pred[512,512]{0,1:T(8,128)(4,1)}, u32[]{:S(2)}) copy-start(pred[512,512]{0,1:T(8,128)(4,1)} %copy-done.8) | copy-start | bytes 786436
  509.3 26.4 %copy-start.78 = (f32[3,512]{1,0:T(4,128)S(1)}, f32[3,512]{1,0:T(4,128)}, u32[]{:S(2)}) copy-start(f32[3,512]{1,0:T(4,128)} %get-tuple-element.347) | copy-start | bytes 18436
  511.1 211.5 %reduce-scatter.25.cloned.1.call-start = ((), (), s32[]{:S(2)}) async-start(), calls=%async_computation.17 | async-start | bytes 983040 | tf_op jit(solution)/shard_map/reduce_scatter | solution.py:213
  518.1 15.3 %collective-permute-start.2 = (bf16[128,768]{1,0:T(8,128)(2,1)}, bf16[128,768]{1,0:T(8,128)(2,1)S(1)}, u32[]{:S(2)}, u32[]{:S(2)}) collective-permute-start(bf16[128,768]{1,0:T(8,128)(2,1)} %collective-permute-done), channel_id=1, source_target_pairs={{0,1},{1,2},{2,3},{3,0},{4,5},{5,6},{6,7},{7,4},{8,9},{9,10},{10,1... | collective-permute-start | bytes 589832 | tf_op jit(solution)/shard_map/ppermute | solution.py:24
  540.8 55.8 %copy-start.1 = (f32[384,768]{1,0:T(8,128)S(1)}, f32[384,768]{1,0:T(8,128)}, u32[]{:S(2)}) copy-start(f32[384,768]{1,0:T(8,128)} %copy-done) | copy-start | bytes 3538948
  540.8 55.8 %copy-start.7 = (f32[384,768]{1,0:T(8,128)S(1)}, f32[384,768]{1,0:T(8,128)}, u32[]{:S(2)}) copy-start(f32[384,768]{1,0:T(8,128)} %copy-done.6) | copy-start | bytes 3538948
  542.6 181.8 %reduce-scatter.33.cloned.1.call-start = ((), (), s32[]{:S(2)}) async-start(), calls=%async_computation.22 | async-start | bytes 245760
  601.2 4.7 copy-start.103
  601.2 22.0 %copy-start.27 = (bf16[384,768]{1,0:T(8,128)(2,1)S(1)}, bf16[384,768]{1,0:T(8,128)(2,1)}, u32[]{:S(2)}) copy-start(bf16[384,768]{1,0:T(8,128)(2,1)} %get-tuple-element.549) | copy-start | bytes 1769476
  602.1 21.1 %collective-permute-start.3 = (bf16[384,768]{1,0:T(8,128)(2,1)S(1)}, bf16[384,768]{1,0:T(8,128)(2,1)}, u32[]{:S(2)}, u32[]{:S(2)}) collective-permute-start(bf16[384,768]{1,0:T(8,128)(2,1)S(1)} %get-tuple-element.312), channel_id=1, source_target_pairs={{0,1},{1,2},{2,3},{3,0},{4,5},{5,6},{6,7},{7,4},{8,9},{9,10},{10,1... | collective-permute-start | bytes 1769480 | tf_op jit(solution)/shard_map/ppermute | solution.py:24
  603.8 31.5 %collective-permute-start.4 = (bf16[384,768]{1,0:T(8,128)(2,1)S(1)}, bf16[384,768]{1,0:T(8,128)(2,1)}, u32[]{:S(2)}, u32[]{:S(2)}) collective-permute-start(bf16[384,768]{1,0:T(8,128)(2,1)S(1)} %get-tuple-element.312), channel_id=1, source_target_pairs={{0,3},{1,0},{2,1},{3,2},{4,7},{5,4},{6,5},{7,6},{8,11},{9,8},{10,9... | collective-permute-start | bytes 1769480 | tf_op jit(solution)/shard_map/ppermute | solution.py:27
  623.2 26.9 %collective-permute-start.5 = (bf16[384,768]{1,0:T(8,128)(2,1)}, bf16[384,768]{1,0:T(8,128)(2,1)}, u32[]{:S(2)}, u32[]{:S(2)}) collective-permute-start(bf16[384,768]{1,0:T(8,128)(2,1)} %collective-permute-done.3), channel_id=1, source_target_pairs={{0,1},{1,2},{2,3},{3,0},{4,5},{5,6},{6,7},{7,4},{8,9},{9,10},{10,1... | collective-permute-start | bytes 1769480 | tf_op jit(solution)/shard_map/ppermute | solution.py:24
  625.2 169.5 %reduce-scatter.29.cloned.1.call-start = ((), (), s32[]{:S(2)}) async-start(), calls=%async_computation.20 | async-start | bytes 2949120 | tf_op jit(solution)/shard_map/reduce_scatter | solution.py:213
  625.2 26.9 %copy-start.57 = (bf16[2,192,768]{2,1,0:T(8,128)(2,1)S(1)}, bf16[2,192,768]{2,1,0:T(8,128)(2,1)}, u32[]{:S(2)}) copy-start(bf16[2,192,768]{2,1,0:T(8,128)(2,1)} %param.40) | copy-start | bytes 1769476
  693.3 245.3 %all-reduce.5.cloned.1.call-start = ((), (), s32[]{:S(2)}) async-start(), calls=%async_computation.23 | async-start | bytes 28311552 | tf_op jit(solution)/shard_map/psum | solution.py:288
  702.0 4.1 copy-start.22
  710.6 3.6 copy-start.111
  720.0 4.2 copy-start.83
  720.0 4.2 copy-start.82
  720.1 4.2 copy-start.91
  720.1 6.0 copy-start.101
  720.1 6.0 copy-start.93
  720.1 6.0 copy-start.92
  938.6 3.5 copy-start.39
  938.6 4.5 copy-start.38
  941.1 3.6 copy-start.12
  943.2 3.8 slice-start
  (82 other events, 123.5 us)
Sparse Core Ops, SparseCore 0:
  9.6 52.6 all-gather.3
  84.8 84.0 reduce-scatter.18
  172.6 55.8 all-gather.5
  230.7 35.1 reduce-scatter.14
  268.6 92.7 reduce-scatter.20
  363.6 36.3 reduce-scatter.16
  402.1 58.8 all-gather.7
  463.3 35.1 reduce-scatter.22
  501.3 95.2 reduce-scatter.26
  598.7 27.2 reduce-scatter.30
  628.3 33.0 reduce-scatter.24
  663.5 19.2 reduce-scatter.32
  693.4 48.9 reduce-scatter.28
  748.7 189.8 all-reduce.4
